TPU v7x, 256 devices: a whole 4x4x8 slice. The times are simulated.
256 devices in a mesh: row: 16 (over z_lo, x, core), col: 4 (over y), item: 4 (over z_hi).
Axes of the slice: x: 4, y: 4, z: 8 (z_hi: 4, z_lo: 2; z = z_hi * 2 + z_lo), core: 2. Of those that a mesh axis runs over, the one named last changes fastest.
Arguments:
- tokens: bfloat16 [4, 16, 64, 2432], P('item', 'row', 'col'), may hold values from -6 to 6
- text_keys_values: bfloat16 [4, 154, 2, 2048], P('item', None, None, 'row'), may hold values from -200 to 200
- text_length: int32 [4], P('item'), may hold values from 2 to 154, as said below
- modulation: float32 [4, 8, 2432], P('item'), may hold values from -4 to 4
- input_weight: bfloat16 [2432, 3, 2048], P(None, None, 'row'), may hold values from -0.125 to 0.125
- norm_gain: float32 [2, 64], replicated, may hold values from 1 to 3
- output_weight: bfloat16 [2048, 2432], P('row'), may hold values from -0.125 to 0.125
- up_weight: bfloat16 [2432, 9728], P(None, 'row'), may hold values from -0.125 to 0.125
- down_weight: bfloat16 [9728, 2432], P('row'), may hold values from -0.0625 to 0.0625
- final_weight: bfloat16 [2432, 64], replicated, may hold values from -0.125 to 0.125
- step_index: int32 [1], replicated, may hold values from 0 to 27
- latent: float32 [4, 16, 4096], P('item', 'row', 'col'), may hold values from -6 to 6
Outputs:
- tokens_out: bfloat16 [4, 16, 64, 2432], P('item', 'row', 'col')
- velocity: float32 [4, 16, 4096], P('item', 'row', 'col')
- latent_next: float32 [4, 16, 4096], P('item', 'row', 'col')
Inputs may be any that keep to these rules, and one draw needn't show every extreme that they name: `text_length`: at least one sequence has all 154 text tokens valid.
All inputs are finite; a program needn't handle non-finite values.
Results may differ from a plain program's by a relative error of at most 0.024.
Values may be sent and summed in bfloat16 or wider, within the bound.
A program may use at most 64 MiB of HBM per device.

v0:
```python
import jax
import jax.numpy as jnp
from jax import lax
from jax.sharding import PartitionSpec as P

HD = 64
STEPS = 28
EPSILON = 1e-06
SHIFT_FACTOR = 3.0
GUIDANCE = 4.5
MASKED = -1e30


def partner_2(value, axis, apart):
    mask = 2**apart
    pairs = [(source, source ^ mask) for source in range(lax.axis_size(axis))]
    return lax.ppermute(value, axis, pairs)


def layer_norm(values):
    center = values - jnp.mean(values, axis=-1, keepdims=True)
    spread = jnp.mean(center * center, axis=-1, keepdims=True)
    return center * lax.rsqrt(spread + EPSILON)


def modulate(values, shift_term, scale_term):
    return (layer_norm(values) * (1.0 + scale_term) + shift_term).astype(jnp.bfloat16)


def root_norm(values, gain_row):
    return (
        values * lax.rsqrt(jnp.mean(values * values, axis=-1, keepdims=True) + EPSILON) * gain_row
    )


def noise_level(position):
    linear = 1.0 - position / STEPS
    return SHIFT_FACTOR * linear / (1.0 + (SHIFT_FACTOR - 1.0) * linear)


def on_device(
    tokens,
    text_keys_values,
    text_length,
    modulation,
    input_weight,
    norm_gain,
    output_weight,
    up_weight,
    down_weight,
    final_weight,
    step_index,
    latent,
):
    tile_rows = tokens.shape[1] * tokens.shape[2]
    model_width = tokens.shape[3]
    mod_rows = modulation[0]
    row_position = lax.axis_index("row")
    stripe_tokens = lax.all_gather(tokens, "row", axis=1, tiled=True)
    stripe_states = stripe_tokens.reshape(-1, model_width).astype(jnp.float32)
    stripe_rows = stripe_states.shape[0]
    local_width = input_weight.shape[2]
    local_heads = local_width // HD
    attn_input = modulate(stripe_states, mod_rows[0], mod_rows[1])
    projected = jnp.dot(
        attn_input,
        input_weight.reshape(model_width, 3 * local_width),
        preferred_element_type=jnp.float32,
    )
    projected = projected.reshape(stripe_rows, 3, local_heads, HD)
    queries = root_norm(projected[:, 0], norm_gain[0]).astype(jnp.bfloat16).transpose(1, 0, 2)
    keys_image = (
        root_norm(projected[:, 1], norm_gain[1])
        .astype(jnp.bfloat16)
        .reshape(stripe_rows, local_width)
    )
    values_image = projected[:, 2].astype(jnp.bfloat16).reshape(stripe_rows, local_width)
    text_pairs = text_keys_values[0]
    keys_text = text_pairs[:, 0].reshape(-1, local_heads, HD)
    values_text = text_pairs[:, 1].reshape(-1, local_heads, HD)
    text_valid = jnp.arange(keys_text.shape[0]) < text_length[0]
    text_scores = jnp.einsum(
        "hsd,thd->hst", queries, keys_text, preferred_element_type=jnp.float32
    ) * HD ** (-0.5)
    text_scores = jnp.where(text_valid[None, None, :], text_scores, MASKED)
    largest = jnp.max(text_scores, axis=-1)
    text_weights = jnp.exp(text_scores - largest[..., None])
    total_mass = jnp.sum(text_weights, axis=-1)
    weighted = jnp.einsum(
        "hst,thd->hsd",
        text_weights.astype(jnp.bfloat16),
        values_text,
        preferred_element_type=jnp.float32,
    )

    def one_block(running, block_pair):
        running_max, running_mass, running_sum = running
        key_block, value_block = block_pair
        scores = jnp.einsum(
            "hsd,khd->hsk", queries, key_block, preferred_element_type=jnp.float32
        ) * HD ** (-0.5)
        new_max = jnp.maximum(running_max, jnp.max(scores, axis=-1))
        factor = jnp.exp(running_max - new_max)
        weights = jnp.exp(scores - new_max[..., None])
        new_mass = running_mass * factor + jnp.sum(weights, axis=-1)
        new_sum = running_sum * factor[..., None] + jnp.einsum(
            "hsk,khd->hsd",
            weights.astype(jnp.bfloat16),
            value_block,
            preferred_element_type=jnp.float32,
        )
        return ((new_max, new_mass, new_sum), None)

    key_piece = lax.all_gather(keys_image, "col", axis=0, tiled=True)
    value_piece = lax.all_gather(values_image, "col", axis=0, tiled=True)
    blocks = key_piece.shape[0] // stripe_rows
    key_blocks = key_piece.reshape(blocks, stripe_rows, local_heads, HD)
    value_blocks = value_piece.reshape(blocks, stripe_rows, local_heads, HD)
    result, unused = lax.scan(
        one_block, (largest, total_mass, weighted), (key_blocks, value_blocks)
    )
    largest, total_mass, weighted = result
    attended = (
        (weighted / total_mass[..., None])
        .astype(jnp.bfloat16)
        .transpose(1, 0, 2)
        .reshape(stripe_rows, local_width)
    )
    attention = lax.psum(
        jnp.dot(attended, output_weight, preferred_element_type=jnp.float32).astype(jnp.bfloat16),
        "row",
    ).astype(jnp.float32)
    stripe_middle = stripe_states + mod_rows[2] * attention
    feed_input = modulate(stripe_middle, mod_rows[3], mod_rows[4])
    hidden = jax.nn.gelu(
        jnp.dot(feed_input, up_weight, preferred_element_type=jnp.float32), approximate=True
    ).astype(jnp.bfloat16)
    middle = lax.dynamic_slice_in_dim(stripe_middle, row_position * tile_rows, tile_rows, 0)
    feed = lax.psum_scatter(
        jnp.dot(hidden, down_weight, preferred_element_type=jnp.float32).astype(jnp.bfloat16),
        "row",
        scatter_dimension=0,
        tiled=True,
    ).astype(jnp.float32)
    leaving = middle + mod_rows[5] * feed
    tokens_out = leaving.astype(jnp.bfloat16).reshape(tokens.shape)
    final_input = modulate(leaving, mod_rows[6], mod_rows[7])
    raw_velocity = jnp.dot(final_input, final_weight, preferred_element_type=jnp.float32).reshape(
        1, tokens.shape[1], -1
    )
    partner = partner_2(raw_velocity, "item", 0)
    is_guided = lax.axis_index("item") % 2 == 0
    guided = jnp.where(is_guided, raw_velocity, partner)
    unguided = jnp.where(is_guided, partner, raw_velocity)
    velocity = unguided + GUIDANCE * (guided - unguided)
    position = step_index[0].astype(jnp.float32)
    step_size = noise_level(position + 1.0) - noise_level(position)
    return (tokens_out, velocity, latent + step_size * velocity)


def solution(mesh):
    in_specs = (
        P("item", "row", "col", None),
        P("item", None, None, "row"),
        P("item"),
        P("item", None, None),
        P(None, None, "row"),
        P(),
        P("row", None),
        P(None, "row"),
        P("row", None),
        P(),
        P(),
        P("item", "row", "col"),
    )
    out_specs = (P("item", "row", "col", None), P("item", "row", "col"), P("item", "row", "col"))
    return jax.shard_map(
        on_device, mesh=mesh, in_specs=in_specs, out_specs=out_specs, check_vma=False
    )
```

profile of v0, /device:TPU:8, one launch (start us, length us, event | category | flops | bytes accessed | tf_op | source)
XLA Modules:
  0.0 311.7 jit_solution(12788335768457517483)
XLA Ops:
  7.3 0.7 all-gather.2.cloned.1.call-update
  8.0 4.1 %copy.26 = bf16[2432,3,128]{0,2,1:T(8,128)(2,1)} copy(bf16[2432,3,128]{2,0,1:T(8,128)(2,1)} %param.18) | data formatting | bytes 3735552 | tf_op args[4]
  13.2 0.7 add_reduce_fusion
  13.9 34.3 %all-gather.2.cloned.1.call-done = bf16[1,16,16,2432]{3,2,0,1:T(8,128)(2,1)} async-done(((bf16[1,1,16,2432]{3,2,0,1:T(8,128)(2,1)}), bf16[1,16,16,2432]{3,2,0,1:T(8,128)(2,1)}) %all-gather.2.cloned.1.call-update) | async-done | bytes 1245200 | tf_op jit(solution)/shard_map/all_gather | solution.py:59
  48.2 1.7 convert_reduce_fusion
  49.9 1.7 multiply_reduce_fusion.1
  51.7 0.6 add_convert_fusion.1
  52.3 0.7 fusion.55
  53.8 12.6 %all_gather.10 = bf16[1024,128]{0,1:T(8,128)(2,1)S(1)} all-gather(bf16[256,128]{0,1:T(8,128)(2,1)S(1)} %fusion.35), channel_id=1, replica_groups=mesh['row'=16,'col'=4,'item'=4] {'col'}, dimensions={0}, use_global_device_ids=true | all-gather | bytes 327680 | tf_op jit(solution)/shard_map/all_gather | solution.py:114
  66.4 0.9 reshape.190
  67.3 1.0 copy.29
  68.3 13.0 %all_gather.11 = bf16[1024,128]{0,1:T(8,128)(2,1)} all-gather(bf16[256,128]{0,1:T(8,128)(2,1)S(1)} %bitcast.82), channel_id=1, replica_groups=mesh['row'=16,'col'=4,'item'=4] {'col'}, dimensions={0}, use_global_device_ids=true | all-gather | bytes 327680 | tf_op jit(solution)/shard_map/all_gather | solution.py:115
  81.3 1.8 reshape.191
  83.1 1.7 copy.30
  84.8 6.1 %while.14 = (s32[]{:T(128)}, f32[2,256]{1,0:T(2,128)S(1)}, f32[2,256]{1,0:T(2,128)S(1)}, f32[2,256,64]{1,2,0:T(8,128)S(1)}, bf16[4,256,2,64]{1,3,2,0:T(8,128)(2,...) while((s32[]{:T(128)}, f32[2,256]{1,0:T(2,128)S(1)}, ...), condition=%wide.region_9.10_spmd, body=%wide.region_6.9_spmd.sunk | while | flops 34407424 | bytes 2064985 | solution.py:119
  85.2 1.1 convolution_add_fusion.2
  86.8 1.1 convolution_add_fusion.2
  88.3 1.1 convolution_add_fusion.2
  89.8 1.1 convolution_add_fusion.2
  91.0 2.7 convolution_convert_fusion
  93.7 124.3 %all-reduce.2.cloned.1.call-done = bf16[256,2432]{1,0:T(8,128)(2,1)} async-done(((bf16[256,2432]{1,0:T(8,128)(2,1)}), bf16[256,2432]{1,0:T(8,128)(2,1)}) %all-reduce.2.cloned.1.call-update) | async-done | bytes 1245200 | tf_op jit(solution)/shard_map/psum | solution.py:129
  218.0 2.2 fusion.51
  220.2 1.4 copy-done.2
  221.6 0.4 multiply_reduce_fusion
  222.0 7.5 %convolution_convert_fusion.1 = bf16[256,2432]{1,0:T(8,128)(2,1)} fusion(bf16[608,2432]{1,0:T(8,128)(2,1)S(1)} %copy-done, bf16[2432,608]{0,1:T(8,128)(2,1)} %param.21, f32[256,2432]{1,0:T(8,128)} %copy-done.2, f32[2432]{0:T(1024)S(1)} %get-tuple-element.58, f32[2432]{0:T(1024)S(1)} %copy-done.7, f32[256]{0:T(256)S(1)} %add_rsqrt_fusion.3, ...), kind=kOutput, calls=%fused_computation.16 | convolution fusion | flops 1519280128 | bytes 9671680 | tf_op jit(solution)/shard_map/dot_general | solution.py:140
  229.6 66.3 %reduce-scatter.2.cloned.1.call-done = bf16[16,2432]{1,0:T(8,128)(2,1)} async-done(((bf16[256,2432]{1,0:T(8,128)(2,1)}), bf16[16,2432]{1,0:T(8,128)(2,1)}) %reduce-scatter.2.cloned.1.call-update) | async-done | bytes 77840 | tf_op jit(solution)/shard_map/reduce_scatter | solution.py:139
  295.9 1.1 fusion.49
  297.0 1.7 multiply_reduce_fusion.2
  298.7 1.2 fusion.36
  300.0 2.6 collective-permute-start
  303.3 1.2 collective-permute-done
  304.6 0.6 multiply_add_fusion.2
  (69 shorter events, 3.2 us)
Async XLA Ops:
  7.2 214.8 %copy-start = (bf16[608,2432]{1,0:T(8,128)(2,1)S(1)}, bf16[608,2432]{1,0:T(8,128)(2,1)}, u32[]{:S(2)}) copy-start(bf16[608,2432]{1,0:T(8,128)(2,1)} %param.22) | copy-start | bytes 8871940
  7.2 4.9 %copy-start.4 = (bf16[1,154,2,128]{3,2,1,0:T(2,128)(2,1)S(1)}, bf16[1,154,2,128]{3,2,1,0:T(2,128)(2,1)}, u32[]{:S(2)}) copy-start(bf16[1,154,2,128]{3,2,1,0:T(2,128)(2,1)} %param.15) | copy-start | bytes 236548
  7.2 5.9 %copy-start.9 = (f32[2,64]{1,0:T(2,128)S(1)}, f32[2,64]{1,0:T(2,128)}, u32[]{:S(2)}) copy-start(f32[2,64]{1,0:T(2,128)} %param.19) | copy-start | bytes 1540
  7.2 6.0 %copy-start.6 = (f32[1,8,2432]{2,1,0:T(8,128)S(1)}, f32[1,8,2432]{2,1,0:T(8,128)}, u32[]{:S(2)}) copy-start(f32[1,8,2432]{2,1,0:T(8,128)} %param.17) | copy-start | bytes 233476
  7.2 41.0 %all-gather.2.cloned.1.call-start = ((), (), s32[]{:S(2)}) async-start(), calls=%async_computation.1 | async-start | bytes 1323008 | tf_op jit(solution)/shard_map/all_gather | solution.py:59
  7.9 210.0 %all-reduce.2.cloned.1.call-start = ((), (), s32[]{:S(2)}) async-start(), calls=%async_computation.2 | async-start | bytes 2490368 | tf_op jit(solution)/shard_map/psum | solution.py:129
  48.2 3.5 %copy-start.1 = (bf16[1,16,16,2432]{3,2,0,1:T(8,128)(2,1)S(1)}, bf16[1,16,16,2432]{3,2,0,1:T(8,128)(2,1)}, u32[]{:S(2)}) copy-start(bf16[1,16,16,2432]{3,2,0,1:T(8,128)(2,1)} %all-gather.2.cloned.1.call-done) | copy-start | bytes 3735556
  48.2 4.1 %copy-start.3 = (bf16[2432,3,128]{0,2,1:T(8,128)(2,1)S(1)}, bf16[2432,3,128]{0,2,1:T(8,128)(2,1)}, u32[]{:S(2)}) copy-start(bf16[2432,3,128]{0,2,1:T(8,128)(2,1)} %copy.26) | copy-start | bytes 5603332
  93.6 202.3 %reduce-scatter.2.cloned.1.call-start = ((), (), s32[]{:S(2)}) async-start(), calls=%async_computation.3 | async-start | bytes 1323008 | tf_op jit(solution)/shard_map/reduce_scatter | solution.py:139
  220.1 1.4 copy-start.2
  220.2 1.9 copy-start.7
  222.0 76.7 %copy-start.5 = (bf16[2432,64]{0,1:T(8,128)(2,1)S(1)}, bf16[2432,64]{0,1:T(8,128)(2,1)}, u32[]{:S(2)}) copy-start(bf16[2432,64]{0,1:T(8,128)(2,1)} %param.23) | copy-start | bytes 933892
  229.5 75.0 %copy-start.8 = (f32[1,1,1024]{2,1,0:T(1,128)S(1)}, f32[1,1,1024]{2,1,0:T(1,128)}, u32[]{:S(2)}) copy-start(f32[1,1,1024]{2,1,0:T(1,128)} %param.25) | copy-start | bytes 12292
  300.0 4.5 %collective-permute-start = (f32[1,1,1024]{2,1,0:T(1,128)S(1)}, f32[1,1,1024]{2,1,0:T(1,128)S(1)}, u32[]{:S(2)}, u32[]{:S(2)}) collective-permute-start(f32[1,1,1024]{2,1,0:T(1,128)S(1)} %reshape.194), channel_id=1, source_target_pairs={{0,1},{1,0},{2,3},{3,2},{4,5},{5,4},{6,7},{7,6},{8,9},{9,8},{10,11... | collective-permute-start | bytes 12296 | tf_op jit(solution)/shard_map/ppermute | solution.py:17
Sparse Core Ops, SparseCore 0:
  9.9 38.2 all-gather.1
  93.8 124.1 all-reduce.1
  229.7 66.1 reduce-scatter.1
where the time goes:
time: 312 us
  waiting for transfers between devices  227 us (73%)
  blocking collectives  25.6 us (8%)
  matrix products  18 us (6%)
  between operations  15.4 us (5%)
  local copies, waits for them, and re-layouts  11.5 us (4%)
  other arithmetic  11.5 us (4%)
    psum x1, waiting for transfers between devices, on_device(): lax.psum(jnp.dot(attended, output_weight, preferred_element_type=jnp.floa...  124 us
    reduce_scatter x1, waiting for transfers between devices, on_device(): lax.psum_scatter(jnp.dot(hidden, down_weight, preferred_element_type=jnp....  66.3 us
    all_gather x1, waiting for transfers between devices, on_device(): stripe_tokens = lax.all_gather(tokens, 'row', axis=1, tiled=True)  34.3 us
    all_gather x1, blocking collectives, on_device(): value_piece = lax.all_gather(values_image, 'col', axis=0, tiled=True)  13 us
    all_gather x1, blocking collectives, on_device(): key_piece = lax.all_gather(keys_image, 'col', axis=0, tiled=True)  12.6 us
    dot_general x1, matrix products, on_device(): jnp.dot(hidden, down_weight, preferred_element_type=jnp.float32)  7.51 us
  transfers between devices with their start and end apart: 4, of which 4 were waited for; matrix products, arithmetic and copies ran while one was open for 2% of the time, Pallas kernels for 0%

commit v1 on v0

--- a/solution.py
+++ b/solution.py
@@ -111,8 +111,13 @@
         )
         return ((new_max, new_mass, new_sum), None)
 
-    key_piece = lax.all_gather(keys_image, "col", axis=0, tiled=True)
-    value_piece = lax.all_gather(values_image, "col", axis=0, tiled=True)
+    key_piece, value_piece = jnp.split(
+        lax.all_gather(
+            jnp.concatenate([keys_image, values_image], axis=1), "col", axis=0, tiled=True
+        ),
+        [keys_image.shape[1]],
+        axis=1,
+    )
     blocks = key_piece.shape[0] // stripe_rows
     key_blocks = key_piece.reshape(blocks, stripe_rows, local_heads, HD)
     value_blocks = value_piece.reshape(blocks, stripe_rows, local_heads, HD)

time: 312 us -> 301 us (0.965)
  blocking collectives: 25.6 us -> 13.5 us
    all_gather x2 -> x1, blocking collectives: 25.6 us -> 13.5 us  [on_device(): lax.all_gather(jnp.concatenate([keys_image, values_image], axis=1), 'col'...]
where the time goes in v1:
time: 301 us; the launch traced here: 300 us
  waiting for transfers between devices  228 us (76%)
  matrix products  18 us (6%)
  between operations  15.4 us (5%)
  blocking collectives  13.5 us (4%)
  local copies, waits for them, and re-layouts  12.2 us (4%)
  other arithmetic  11 us (4%)
    psum x1, waiting for transfers between devices, on_device(): lax.psum(jnp.dot(attended, output_weight, preferred_element_type=jnp.floa...  124 us
    reduce_scatter x1, waiting for transfers between devices, on_device(): lax.psum_scatter(jnp.dot(hidden, down_weight, preferred_element_type=jnp....  66.3 us
    all_gather x1, waiting for transfers between devices, on_device(): stripe_tokens = lax.all_gather(tokens, 'row', axis=1, tiled=True)  34.8 us
    all_gather x1, blocking collectives, on_device(): lax.all_gather(jnp.concatenate([keys_image, values_image], axis=1), 'col'...  13.5 us
    dot_general x1, matrix products, on_device(): jnp.dot(hidden, down_weight, preferred_element_type=jnp.float32)  7.51 us
  transfers between devices with their start and end apart: 4, of which 4 were waited for; matrix products, arithmetic and copies ran while one was open for 2% of the time, Pallas kernels for 0%

profile of v1, /device:TPU:8, one launch (start us, length us, event | category | flops | bytes accessed | tf_op | source)
XLA Modules:
  0.0 300.3 jit_solution(9170764886882312194)
XLA Ops:
  7.3 0.7 all-gather.2.cloned.1.call-update
  8.0 4.1 %copy.26 = bf16[2432,3,128]{0,2,1:T(8,128)(2,1)} copy(bf16[2432,3,128]{2,0,1:T(8,128)(2,1)} %param.18) | data formatting | bytes 3735552 | tf_op args[4]
  13.4 34.8 %all-gather.2.cloned.1.call-done = bf16[1,16,16,2432]{3,2,0,1:T(8,128)(2,1)} async-done(((bf16[1,1,16,2432]{3,2,0,1:T(8,128)(2,1)}), bf16[1,16,16,2432]{3,2,0,1:T(8,128)(2,1)}) %all-gather.2.cloned.1.call-update) | async-done | bytes 1245200 | tf_op jit(solution)/shard_map/all_gather | solution.py:59
  48.2 1.7 convert_reduce_fusion
  49.9 1.7 multiply_reduce_fusion.1
  51.7 0.6 add_convert_fusion.1
  52.3 0.7 fusion.56
  53.8 13.5 %all_gather.7 = bf16[1024,256]{0,1:T(8,128)(2,1)S(1)} all-gather(bf16[256,256]{0,1:T(8,128)(2,1)S(1)} %pad_maximum_fusion), channel_id=1, replica_groups=mesh['row'=16,'col'=4,'item'=4] {'col'}, dimensions={0}, use_global_device_ids=true | all-gather | bytes 655360 | tf_op jit(solution)/shard_map/all_gather | solution.py:115
  67.3 0.7 fusion.53
  68.0 0.9 reshape.190
  68.9 1.0 copy.29
  69.9 1.8 reshape.191
  71.7 1.7 copy.30
  73.4 6.1 %while.14 = (s32[]{:T(128)}, f32[2,256]{1,0:T(2,128)S(1)}, f32[2,256]{1,0:T(2,128)S(1)}, f32[2,256,64]{1,2,0:T(8,128)S(1)}, bf16[4,256,2,64]{1,3,2,0:T(8,128)(2,...) while((s32[]{:T(128)}, f32[2,256]{1,0:T(2,128)S(1)}, ...), condition=%wide.region_9.10_spmd, body=%wide.region_6.9_spmd.sunk | while | flops 34407424 | bytes 2064985 | solution.py:124
  73.8 1.1 convolution_add_fusion.2
  74.9 0.3 fusion.76
  75.3 1.1 convolution_add_fusion.2
  76.9 1.1 convolution_add_fusion.2
  78.4 1.1 convolution_add_fusion.2
  79.5 2.7 convolution_convert_fusion
  82.3 124.3 %all-reduce.2.cloned.1.call-done = bf16[256,2432]{1,0:T(8,128)(2,1)} async-done(((bf16[256,2432]{1,0:T(8,128)(2,1)}), bf16[256,2432]{1,0:T(8,128)(2,1)}) %all-reduce.2.cloned.1.call-update) | async-done | bytes 1245200 | tf_op jit(solution)/shard_map/psum | solution.py:134
  206.5 2.2 fusion.51
  208.7 1.4 copy-done.2
  210.1 0.4 multiply_reduce_fusion
  210.6 7.5 %convolution_convert_fusion.1 = bf16[256,2432]{1,0:T(8,128)(2,1)} fusion(bf16[608,2432]{1,0:T(8,128)(2,1)S(1)} %copy-done, bf16[2432,608]{0,1:T(8,128)(2,1)} %param.21, f32[256,2432]{1,0:T(8,128)} %copy-done.2, f32[2432]{0:T(1024)S(1)} %get-tuple-element.58, f32[2432]{0:T(1024)S(1)} %get-tuple-element.59, f32[256]{0:T(256)S(1)} %add_rsqrt_fusion.3, ...), kind=kOutput, calls=%fused_computation.16 | convolution fusion | flops 1519280128 | bytes 9671680 | tf_op jit(solution)/shard_map/dot_general | solution.py:145
  218.1 66.3 %reduce-scatter.2.cloned.1.call-done = bf16[16,2432]{1,0:T(8,128)(2,1)} async-done(((bf16[256,2432]{1,0:T(8,128)(2,1)}), bf16[16,2432]{1,0:T(8,128)(2,1)}) %reduce-scatter.2.cloned.1.call-update) | async-done | bytes 77840 | tf_op jit(solution)/shard_map/reduce_scatter | solution.py:144
  284.5 1.1 fusion.49
  285.5 1.7 multiply_reduce_fusion.2
  287.3 1.2 fusion.36
  288.6 2.4 collective-permute-start
  291.7 1.4 collective-permute-done
  293.1 0.6 multiply_add_fusion.2
  (68 shorter events, 3.1 us)
Async XLA Ops:
  7.2 203.4 %copy-start = (bf16[608,2432]{1,0:T(8,128)(2,1)S(1)}, bf16[608,2432]{1,0:T(8,128)(2,1)}, u32[]{:S(2)}) copy-start(bf16[608,2432]{1,0:T(8,128)(2,1)} %param.22) | copy-start | bytes 8871940
  7.2 4.9 %copy-start.4 = (bf16[1,154,2,128]{3,2,1,0:T(2,128)(2,1)S(1)}, bf16[1,154,2,128]{3,2,1,0:T(2,128)(2,1)}, u32[]{:S(2)}) copy-start(bf16[1,154,2,128]{3,2,1,0:T(2,128)(2,1)} %param.15) | copy-start | bytes 236548
  7.2 5.9 %copy-start.8 = (f32[2,64]{1,0:T(2,128)S(1)}, f32[2,64]{1,0:T(2,128)}, u32[]{:S(2)}) copy-start(f32[2,64]{1,0:T(2,128)} %param.19) | copy-start | bytes 1540
  7.2 6.0 %copy-start.6 = (f32[1,8,2432]{2,1,0:T(8,128)S(1)}, f32[1,8,2432]{2,1,0:T(8,128)}, u32[]{:S(2)}) copy-start(f32[1,8,2432]{2,1,0:T(8,128)} %param.17) | copy-start | bytes 233476
  7.2 41.0 %all-gather.2.cloned.1.call-start = ((), (), s32[]{:S(2)}) async-start(), calls=%async_computation.1 | async-start | bytes 1323008 | tf_op jit(solution)/shard_map/all_gather | solution.py:59
  7.9 198.6 %all-reduce.2.cloned.1.call-start = ((), (), s32[]{:S(2)}) async-start(), calls=%async_computation.2 | async-start | bytes 2490368 | tf_op jit(solution)/shard_map/psum | solution.py:134
  48.2 3.5 %copy-start.1 = (bf16[1,16,16,2432]{3,2,0,1:T(8,128)(2,1)S(1)}, bf16[1,16,16,2432]{3,2,0,1:T(8,128)(2,1)}, u32[]{:S(2)}) copy-start(bf16[1,16,16,2432]{3,2,0,1:T(8,128)(2,1)} %all-gather.2.cloned.1.call-done) | copy-start | bytes 3735556
  48.2 4.1 %copy-start.3 = (bf16[2432,3,128]{0,2,1:T(8,128)(2,1)S(1)}, bf16[2432,3,128]{0,2,1:T(8,128)(2,1)}, u32[]{:S(2)}) copy-start(bf16[2432,3,128]{0,2,1:T(8,128)(2,1)} %copy.26) | copy-start | bytes 5603332
  82.2 202.2 %reduce-scatter.2.cloned.1.call-start = ((), (), s32[]{:S(2)}) async-start(), calls=%async_computation.3 | async-start | bytes 1323008 | tf_op jit(solution)/shard_map/reduce_scatter | solution.py:144
  208.7 1.4 copy-start.2
  210.6 76.7 %copy-start.5 = (bf16[2432,64]{0,1:T(8,128)(2,1)S(1)}, bf16[2432,64]{0,1:T(8,128)(2,1)}, u32[]{:S(2)}) copy-start(bf16[2432,64]{0,1:T(8,128)(2,1)} %param.23) | copy-start | bytes 933892
  218.1 75.0 %copy-start.7 = (f32[1,1,1024]{2,1,0:T(1,128)S(1)}, f32[1,1,1024]{2,1,0:T(1,128)}, u32[]{:S(2)}) copy-start(f32[1,1,1024]{2,1,0:T(1,128)} %param.25) | copy-start | bytes 12292
  288.6 4.5 %collective-permute-start = (f32[1,1,1024]{2,1,0:T(1,128)S(1)}, f32[1,1,1024]{2,1,0:T(1,128)S(1)}, u32[]{:S(2)}, u32[]{:S(2)}) collective-permute-start(f32[1,1,1024]{2,1,0:T(1,128)S(1)} %reshape.194), channel_id=1, source_target_pairs={{0,1},{1,0},{2,3},{3,2},{4,5},{5,4},{6,7},{7,6},{8,9},{9,8},{10,11... | collective-permute-start | bytes 12296 | tf_op jit(solution)/shard_map/ppermute | solution.py:17
Sparse Core Ops, SparseCore 0:
  9.9 38.2 all-gather.1
  82.3 124.1 all-reduce.1
  218.2 66.1 reduce-scatter.1
